TPU v7x, 32 devices: a whole 2x2x4 slice. The times are simulated.
32 devices in a mesh: row: 8 (over y, x, core), col: 4 (over z).
Axes of the slice: x: 2, y: 2, z: 4, core: 2. Of those that a mesh axis runs over, the one named last changes fastest.
Arguments:
- key_rows: float32 [128, 20480], P('col', 'row'), may hold values from -0.0390625 to 0.0390625
- targets: float32 [128, 7168], P(None, 'col'), may hold values from -24 to 24
- weight: float32 [20480, 7168], P('row', 'col'), may hold values from -6 to 6
- covariance: float32 [20480, 20480], P('row', 'col'), may hold values from -3 to 24, as said below
Outputs:
- increment: float32 [20480, 7168], P('row', 'col')
Inputs may be any that keep to these rules, and one draw needn't show every extreme that they name: covariance is symmetric and positive definite.
All inputs are finite; a program needn't handle non-finite values.
Results may differ from a plain program's by a relative error of at most 0.0003.
Values sent between devices are 32-bit elements; how exact they have to be, the bound alone decides.
No kernel may reach another device: no remote copies, remote signals or barrier semaphores. Data moves between devices by JAX's collectives and lax.ppermute only.
A program may use at most 192 MiB of HBM per device.

v0:
```python
import jax
import jax.numpy as jnp
from jax import lax
from jax.sharding import PartitionSpec as P


def spread(value, axis, root):
    mine = lax.axis_index(axis) == root
    return lax.psum(jnp.where(mine, value, jnp.zeros_like(value)), axis)


def precise(left, right):
    return jnp.dot(left, right, precision=lax.Precision.HIGHEST, preferred_element_type=jnp.float32)


def transposed_product(left, right):
    return lax.dot_general(
        left,
        right,
        (((0,), (0,)), ((), ())),
        precision=lax.Precision.HIGHEST,
        preferred_element_type=jnp.float32,
    )


def definite_solve(matrix, right_side):
    factor = jnp.linalg.cholesky(0.5 * (matrix + matrix.T))
    return jax.scipy.linalg.cho_solve((factor, True), right_side)


def fetch_panel(local_rows):
    blocks_per = lax.axis_size("row") // lax.axis_size("col")
    col_index = lax.axis_index("col")
    pieces = []
    for part_index in range(blocks_per):
        pieces.append(spread(local_rows, "row", col_index * blocks_per + part_index))
    return jnp.concatenate(pieces, axis=0)


def covariance_rows(covariance, local_rows):
    panel_rows = fetch_panel(local_rows)
    return lax.psum(precise(covariance, panel_rows), "col")


def body(key_rows, targets, weight, covariance):
    all_keys = lax.all_gather(key_rows, "col", axis=0, tiled=True)
    basis_panel = all_keys.T
    fitted, gram_keys = lax.psum((precise(all_keys, weight), precise(all_keys, basis_panel)), "row")
    residual = targets - fitted
    image_one = covariance_rows(covariance, basis_panel) + precise(basis_panel, gram_keys)
    curvature, square = lax.psum(
        (transposed_product(basis_panel, image_one), transposed_product(image_one, image_one)),
        "row",
    )
    alpha_one = definite_solve(curvature, gram_keys)
    residual_next = basis_panel - precise(image_one, alpha_one)
    norm_next = transposed_product(alpha_one, precise(square, alpha_one)) - gram_keys
    beta_one = definite_solve(gram_keys, norm_next)
    direction = residual_next + precise(basis_panel, beta_one)
    key_part = precise(all_keys, direction)
    cov_direction = covariance_rows(covariance, direction)
    key_direction, curve_part = lax.psum(
        (key_part, transposed_product(direction, cov_direction)), "row"
    )
    curvature_two = curve_part + transposed_product(key_direction, key_direction)
    alpha_two = definite_solve(curvature_two, norm_next)
    solved = precise(basis_panel, alpha_one) + precise(direction, alpha_two)
    return precise(solved, residual)


def solution(mesh):
    placed = (P("col", "row"), P(None, "col"), P("row", "col"), P("row", "col"))
    return jax.shard_map(
        body, mesh=mesh, in_specs=placed, out_specs=P("row", "col"), check_vma=False
    )
```

profile of v0, /device:TPU:0, one launch (start us, length us, event | category | flops | bytes accessed | tf_op | source)
XLA Modules:
  0.0 627.3 jit_solution(12307424067801751636)
XLA Ops:
  7.3 37.0 %all-gather.2.cloned.1.call-done = f32[128,2560]{1,0:T(8,128)} async-done(((f32[32,2560]{1,0:T(8,128)}), f32[128,2560]{1,0:T(8,128)}) %all-gather.2.cloned.1.call-update) | async-done | bytes 1310736 | tf_op jit(solution)/shard_map/all_gather | solution.py:46
  50.2 64.8 %all-reduce.21.cloned.1.call-done = (f32[128,128]{1,0:T(8,128)}, f32[2560,128]{1,0:T(8,128)}, f32[2560,128]{1,0:T(8,128)}) async-done(((f32[128,128]{1,0:T(8,128)}, f32[2560,128]{1,0:T(8,128)}, f32[2560,128]{1,0:T(8,128)}), (f32[128,128]{1,0:T(8,128)}, f32[2560,128]{1,0:T(8,128)}, f32[2560,128]{1,0:T(8,128)})) %all-reduce.21.cloned.1.call-update) | async-done | bytes 2686992 | tf_op jit(solution)/shard_map/psum | solution.py:48
  115.1 60.9 %convolution_bitcast_fusion.4 = f32[2560,128]{0,1:T(8,128)} fusion(f32[2560,5120]{1,0:T(8,128)} %param.10, f32[2560,128]{1,0:T(8,128)} %get-tuple-element.15, f32[2560,128]{1,0:T(8,128)} %get-tuple-element.16), kind=kOutput, calls=%fused_computation.8 | convolution fusion | flops 20133314560 | bytes 56360960 | tf_op jit(solution)/shard_map/dot_general | solution.py:13
  177.1 11.7 %cholesky.70 = f32[128,128]{1,0:T(8,128)S(1)} custom-call(f32[128,128]{1,0:T(8,128)S(1)} %fusion.23), custom_call_target="Cholesky" | custom-call | tf_op jit(solution)/shard_map/jit(cholesky)/cholesky | solution.py:27
  189.5 46.5 %all-reduce.11.cloned.1.call-done = f32[2560,128]{0,1:T(8,128)} async-done(((f32[2560,128]{0,1:T(8,128)}), f32[2560,128]{0,1:T(8,128)}) %all-reduce.11.cloned.1.call-update) | async-done | bytes 1310736 | tf_op jit(solution)/shard_map/psum | solution.py:42
  236.0 2.6 fusion.1
  243.4 9.8 %custom-call.10 = f32[1,128,128]{1,2,0:T(8,128)S(1)} custom-call(f32[1,128,128]{2,1,0:T(8,128)S(1)} %fusion.11), custom_call_target="InvertDiagBlocksLowerTriangular" | custom-call | tf_op jit(solution)/shard_map/jit(_cho_solve)/triangular_solve | solution.py:28
  253.2 42.0 %all-reduce.19.cloned.1.call-done = (f32[128,128]{1,0:T(8,128)}, f32[128,128]{1,0:T(8,128)}) async-done(((f32[128,128]{1,0:T(8,128)}, f32[128,128]{1,0:T(8,128)}), (f32[128,128]{1,0:T(8,128)}, f32[128,128]{1,0:T(8,128)})) %all-reduce.19.cloned.1.call-update) | async-done | bytes 131088 | tf_op jit(solution)/shard_map/psum | solution.py:51
  297.1 11.7 %cholesky.59 = f32[128,128]{1,0:T(8,128)S(1)} custom-call(f32[128,128]{1,0:T(8,128)S(1)} %fusion.29), custom_call_target="Cholesky" | custom-call | tf_op jit(solution)/shard_map/jit(cholesky)/cholesky | solution.py:27
  310.1 9.8 %custom-call.9 = f32[1,128,128]{1,2,0:T(8,128)S(1)} custom-call(f32[1,128,128]{2,1,0:T(8,128)S(1)} %fusion.10), custom_call_target="InvertDiagBlocksLowerTriangular" | custom-call | tf_op jit(solution)/shard_map/jit(_cho_solve)/triangular_solve | solution.py:28
  322.3 2.2 convolution_bitcast_fusion
  324.6 4.4 broadcast_select_fusion.1
  329.0 64.2 %all-reduce.17.cloned.1.call-done = (f32[2560,128]{1,0:T(8,128)}, f32[2560,128]{1,0:T(8,128)}) async-done(((f32[2560,128]{1,0:T(8,128)}, f32[2560,128]{1,0:T(8,128)}), (f32[2560,128]{1,0:T(8,128)}, f32[2560,128]{1,0:T(8,128)})) %all-reduce.17.cloned.1.call-update) | async-done | bytes 2621456 | tf_op jit(solution)/shard_map/psum | solution.py:9
  393.2 60.9 %convolution_bitcast_fusion.3 = f32[2560,128]{0,1:T(8,128)} fusion(f32[2560,5120]{1,0:T(8,128)} %param.10, f32[2560,128]{1,0:T(8,128)} %get-tuple-element.10, f32[2560,128]{1,0:T(8,128)} %get-tuple-element.11), kind=kOutput, calls=%fused_computation.7 | convolution fusion | flops 20133314560 | bytes 56360960 | tf_op jit(solution)/shard_map/dot_general | solution.py:13
  454.4 14.2 %fusion.37 = f32[128,1792]{1,0:T(8,128)} fusion(f32[128,2560]{1,0:T(8,128)S(1)} %copy-done, f32[2560,1792]{1,0:T(8,128)} %param.9), kind=kOutput, calls=%fused_computation.69 | convolution fusion | flops 7046430720 | bytes 20578304 | tf_op jit(solution)/shard_map/dot_general | solution.py:13
  468.6 2.9 convolution_bitcast_fusion.5
  471.5 42.5 %all-reduce.13.cloned.1.call-done = f32[2560,128]{0,1:T(8,128)} async-done(((f32[2560,128]{0,1:T(8,128)}), f32[2560,128]{0,1:T(8,128)}) %all-reduce.13.cloned.1.call-update) | async-done | bytes 1310736 | tf_op jit(solution)/shard_map/psum | solution.py:42
  514.0 4.2 fusion.36
  518.2 2.3 convolution_bitcast_fusion.1
  520.5 54.2 %all-reduce.15.cloned.1.call-done = (f32[128,128]{1,0:T(8,128)}, f32[128,128]{0,1:T(8,128)}, f32[128,1792]{1,0:T(8,128)}) async-done(((f32[128,128]{1,0:T(8,128)}, f32[128,128]{0,1:T(8,128)}, f32[128,1792]{1,0:T(8,128)}), (f32[128,128]{1,0:T(8,128)}, f32[128,128]{0,1:T(8,128)}, f32[128,1792]{1,0:T(8,128)})) %all-reduce.15.cloned.1.call-update) | async-done | bytes 1048592 | tf_op jit(solution)/shard_map/psum | solution.py:62
  576.2 11.7 %cholesky.81 = f32[128,128]{1,0:T(8,128)S(1)} custom-call(f32[128,128]{1,0:T(8,128)S(1)} %fusion.17), custom_call_target="Cholesky" | custom-call | tf_op jit(solution)/shard_map/jit(cholesky)/cholesky | solution.py:27
  589.2 9.8 %custom-call.11 = f32[1,128,128]{1,2,0:T(8,128)S(1)} custom-call(f32[1,128,128]{2,1,0:T(8,128)S(1)} %fusion.12), custom_call_target="InvertDiagBlocksLowerTriangular" | custom-call | tf_op jit(solution)/shard_map/jit(_cho_solve)/triangular_solve | solution.py:28
  599.8 2.8 convolution_add_fusion
  602.6 17.4 %fusion.8 = f32[2560,1792]{1,0:T(8,128)} fusion(f32[2560,128]{0,1:T(8,128)S(1)} %convolution_add_fusion, f32[128,1792]{1,0:T(8,128)S(1)} %copy-done.5, f32[128,1792]{1,0:T(8,128)S(1)} %copy-done.6), kind=kOutput, calls=%fused_computation.21 | convolution fusion | flops 7046660096 | bytes 21495808 | tf_op jit(solution)/shard_map/dot_general | solution.py:13
  (63 shorter events, 22.5 us)
Async XLA Ops:
  6.5 37.8 %all-gather.2.cloned.1.call-start = ((), (), s32[]{:S(2)}) async-start(), calls=%async_computation | async-start | bytes 1638400 | tf_op jit(solution)/shard_map/all_gather | solution.py:46
  7.3 107.8 %all-reduce.21.cloned.1.call-start = ((), (), s32[]{:S(2)}) async-start(), calls=%async_computation.6 | async-start | bytes 5373952 | tf_op jit(solution)/shard_map/psum | solution.py:48
  46.1 1.9 copy-start.2
  46.1 2.3 copy-start
  50.2 185.8 %all-reduce.11.cloned.1.call-start = ((), (), s32[]{:S(2)}) async-start(), calls=%async_computation.1 | async-start | bytes 2621440 | tf_op jit(solution)/shard_map/psum | solution.py:42
  176.0 0.8 copy-start.4
  176.0 119.2 %all-reduce.19.cloned.1.call-start = ((), (), s32[]{:S(2)}) async-start(), calls=%async_computation.5 | async-start | bytes 262144 | tf_op jit(solution)/shard_map/psum | solution.py:51
  242.2 151.0 %all-reduce.17.cloned.1.call-start = ((), (), s32[]{:S(2)}) async-start(), calls=%async_computation.4 | async-start | bytes 5242880 | tf_op jit(solution)/shard_map/psum | solution.py:9
  322.3 2.3 copy-start.3
  329.0 185.0 %all-reduce.13.cloned.1.call-start = ((), (), s32[]{:S(2)}) async-start(), calls=%async_computation.2 | async-start | bytes 2621440 | tf_op jit(solution)/shard_map/psum | solution.py:42
  454.2 14.4 %copy-start.1 = (f32[2560,128]{1,0:T(8,128)S(1)}, f32[2560,128]{1,0:T(8,128)}, u32[]{:S(2)}) copy-start(f32[2560,128]{1,0:T(8,128)} %get-tuple-element.21) | copy-start | bytes 3932164
  454.2 120.6 %all-reduce.15.cloned.1.call-start = ((), (), s32[]{:S(2)}) async-start(), calls=%async_computation.3 | async-start | bytes 2097152 | tf_op jit(solution)/shard_map/psum | solution.py:62
  599.8 2.8 copy-start.5
  599.8 2.8 copy-start.6
Sparse Core Ops, SparseCore 0:
  8.9 35.3 all-gather.1
  50.3 64.7 all-reduce.20
  176.1 59.7 all-reduce.10
  242.4 52.7 all-reduce.18
  329.1 64.0 all-reduce.16
  454.3 59.6 all-reduce.12
  518.3 56.3 all-reduce.14
where the time goes:
time: 637 us; the launch traced here: 627 us
  waiting for transfers between devices  352 us (55%)
  matrix products  184 us (29%)
  other arithmetic  71.3 us (11%)
  between operations  14.2 us (2%)
    dot_general x12, matrix products, precise(): jnp.dot(left, right, precision=lax.Precision.HIGHEST, preferred_element_t...  173 us
    psum x2, waiting for transfers between devices, covariance_rows(): return lax.psum(precise(covariance, panel_rows), 'col')  89 us
    psum x1, waiting for transfers between devices, body(): lax.psum((precise(all_keys, weight), precise(all_keys, basis_panel)), 'row')  64.8 us
    psum x1, waiting for transfers between devices, spread(): return lax.psum(jnp.where(mine, value, jnp.zeros_like(value)), axis)  64.2 us
    psum x1, waiting for transfers between devices, body(): lax.psum((key_part, transposed_product(direction, cov_direction)), 'row')  54.2 us
    psum x1, waiting for transfers between devices, body(): lax.psum((transposed_product(basis_panel, image_one), transposed_product(...  42 us
    another operation x9, other arithmetic, definite_solve(): factor = jnp.linalg.cholesky(0.5 * (matrix + matrix.T))  37.3 us
    all_gather x1, waiting for transfers between devices, body(): all_keys = lax.all_gather(key_rows, 'col', axis=0, tiled=True)  37 us
  transfers between devices with their start and end apart: 7, of which 7 were waited for; matrix products, arithmetic and copies ran while one was open for 7% of the time, Pallas kernels for 0%

commit v1 on v0

--- a/solution.py
+++ b/solution.py
@@ -4,9 +4,14 @@
 from jax.sharding import PartitionSpec as P
 
 
+def post_state(u, across):
+    before = lax.all_gather(u, axis_name=across)
+    return jnp.sum(before, axis=0)
+
+
 def spread(value, axis, root):
     mine = lax.axis_index(axis) == root
-    return lax.psum(jnp.where(mine, value, jnp.zeros_like(value)), axis)
+    return post_state(jnp.where(mine, value, jnp.zeros_like(value)), axis)
 
 
 def precise(left, right):

time: 637 us -> 767 us (1.20)
  waiting for transfers between devices: 352 us -> 466 us
  other arithmetic: 71.3 us -> 92.9 us
    all_gather x0 -> x4, waiting for transfers between devices: none -> 242 us  [post_state(): before = lax.all_gather(u, axis_name=across)]
    psum x1, waiting for transfers between devices: 64.8 us -> 0.02 us  [body(): lax.psum((precise(all_keys, weight), precise(all_keys, basis_panel)), 'row')]
    psum x1 -> x0, waiting for transfers between devices: 64.2 us -> none  [spread(): return lax.psum(jnp.where(mine, value, jnp.zeros_like(value)), axis)]
    reduce_sum x0 -> x4, other arithmetic: none -> 20.6 us  [post_state(): return jnp.sum(before, axis=0)]
  transfers between devices with their start and end apart: 7 -> 10, of which waited for: 7 -> 9; matrix products, arithmetic and copies ran while one was open for 7% -> 16% of each run, Pallas kernels for 0% -> 0%
where the time goes in v1:
time: 767 us; the launch traced here: 764 us
  waiting for transfers between devices  466 us (61%)
  matrix products  185 us (24%)
  other arithmetic  92.9 us (12%)
  between operations  14.1 us (2%)
    all_gather x4, waiting for transfers between devices, post_state(): before = lax.all_gather(u, axis_name=across)  242 us
    dot_general x12, matrix products, precise(): jnp.dot(left, right, precision=lax.Precision.HIGHEST, preferred_element_t...  174 us
    psum x2, waiting for transfers between devices, covariance_rows(): return lax.psum(precise(covariance, panel_rows), 'col')  88.1 us
    psum x1, waiting for transfers between devices, body(): lax.psum((key_part, transposed_product(direction, cov_direction)), 'row')  54.2 us
    psum x1, waiting for transfers between devices, body(): lax.psum((transposed_product(basis_panel, image_one), transposed_product(...  42.2 us
    another operation x9, other arithmetic, definite_solve(): factor = jnp.linalg.cholesky(0.5 * (matrix + matrix.T))  37.3 us
    all_gather x1, waiting for transfers between devices, body(): all_keys = lax.all_gather(key_rows, 'col', axis=0, tiled=True)  37 us
    another operation x6, other arithmetic, definite_solve(): return jax.scipy.linalg.cho_solve((factor, True), right_side)  31.4 us
  transfers between devices with their start and end apart: 10, of which 9 were waited for; matrix products, arithmetic and copies ran while one was open for 16% of the time, Pallas kernels for 0%

profile of v1, /device:TPU:0, one launch (start us, length us, event | category | flops | bytes accessed | tf_op | source)
XLA Modules:
  0.0 763.5 jit_solution(13931768302436963449)
XLA Ops:
  7.3 37.0 %all-gather.10.cloned.1.call-done = f32[128,2560]{1,0:T(8,128)} async-done(((f32[32,2560]{1,0:T(8,128)}), f32[128,2560]{1,0:T(8,128)}) %all-gather.10.cloned.1.call-update) | async-done | bytes 1310736 | tf_op jit(solution)/shard_map/all_gather | solution.py:51
  51.2 59.2 %all-gather.12.cloned.1.call-done = f32[20480,128]{1,0:T(8,128)} async-done(((f32[2560,128]{1,0:T(8,128)}), f32[20480,128]{1,0:T(8,128)}) %all-gather.12.cloned.1.call-update) | async-done | bytes 10485776 | tf_op jit(solution)/shard_map/all_gather | solution.py:8
  110.5 4.6 reduce_sum.36
  115.1 60.5 %all-gather.14.cloned.1.call-done = f32[20480,128]{1,0:T(8,128)} async-done(((f32[2560,128]{1,0:T(8,128)}), f32[20480,128]{1,0:T(8,128)}) %all-gather.14.cloned.1.call-update) | async-done | bytes 10485776 | tf_op jit(solution)/shard_map/all_gather | solution.py:8
  175.6 5.7 reduce_sum.37
  181.3 61.1 %convolution_bitcast_fusion.4 = f32[2560,128]{0,1:T(8,128)} fusion(f32[2560,5120]{1,0:T(8,128)} %param.10, f32[2560,128]{1,0:T(8,128)} %reduce_sum.37, f32[2560,128]{1,0:T(8,128)S(1)} %reduce_sum.36), kind=kOutput, calls=%fused_computation.8 | convolution fusion | flops 20133314560 | bytes 56360960 | tf_op jit(solution)/shard_map/dot_general | solution.py:18
  244.9 11.7 %cholesky.70 = f32[128,128]{1,0:T(8,128)S(1)} custom-call(f32[128,128]{1,0:T(8,128)S(1)} %fusion.23), custom_call_target="Cholesky" | custom-call | tf_op jit(solution)/shard_map/jit(cholesky)/cholesky | solution.py:32
  257.4 45.2 %all-reduce.8.cloned.1.call-done = f32[2560,128]{0,1:T(8,128)} async-done(((f32[2560,128]{0,1:T(8,128)}), f32[2560,128]{0,1:T(8,128)}) %all-reduce.8.cloned.1.call-update) | async-done | bytes 1310736 | tf_op jit(solution)/shard_map/psum | solution.py:47
  309.8 9.8 %custom-call.10 = f32[1,128,128]{1,2,0:T(8,128)S(1)} custom-call(f32[1,128,128]{2,1,0:T(8,128)S(1)} %fusion.11), custom_call_target="InvertDiagBlocksLowerTriangular" | custom-call | tf_op jit(solution)/shard_map/jit(_cho_solve)/triangular_solve | solution.py:33
  319.6 42.2 %all-reduce.16.cloned.1.call-done = (f32[128,128]{1,0:T(8,128)}, f32[128,128]{1,0:T(8,128)}) async-done(((f32[128,128]{1,0:T(8,128)}, f32[128,128]{1,0:T(8,128)}), (f32[128,128]{1,0:T(8,128)}, f32[128,128]{1,0:T(8,128)})) %all-reduce.16.cloned.1.call-update) | async-done | bytes 131088 | tf_op jit(solution)/shard_map/psum | solution.py:56
  363.7 11.7 %cholesky.59 = f32[128,128]{1,0:T(8,128)S(1)} custom-call(f32[128,128]{1,0:T(8,128)S(1)} %fusion.29), custom_call_target="Cholesky" | custom-call | tf_op jit(solution)/shard_map/jit(cholesky)/cholesky | solution.py:32
  376.8 9.8 %custom-call.9 = f32[1,128,128]{1,2,0:T(8,128)S(1)} custom-call(f32[1,128,128]{2,1,0:T(8,128)S(1)} %fusion.10), custom_call_target="InvertDiagBlocksLowerTriangular" | custom-call | tf_op jit(solution)/shard_map/jit(_cho_solve)/triangular_solve | solution.py:33
  391.3 4.6 broadcast_select_fusion.1
  396.7 62.0 %all-gather.16.cloned.1.call-done = f32[20480,128]{1,0:T(8,128)} async-done(((f32[2560,128]{1,0:T(8,128)}), f32[20480,128]{1,0:T(8,128)}) %all-gather.16.cloned.1.call-update) | async-done | bytes 10485776 | tf_op jit(solution)/shard_map/all_gather | solution.py:8
  458.7 4.6 reduce_sum.38
  463.3 60.5 %all-gather.18.cloned.1.call-done = f32[20480,128]{1,0:T(8,128)} async-done(((f32[2560,128]{1,0:T(8,128)}), f32[20480,128]{1,0:T(8,128)}) %all-gather.18.cloned.1.call-update) | async-done | bytes 10485776 | tf_op jit(solution)/shard_map/all_gather | solution.py:8
  523.8 5.7 reduce_sum.39
  529.5 60.8 %convolution_bitcast_fusion.3 = f32[2560,128]{0,1:T(8,128)} fusion(f32[2560,5120]{1,0:T(8,128)} %param.10, f32[2560,128]{1,0:T(8,128)} %reduce_sum.39, f32[2560,128]{1,0:T(8,128)S(1)} %reduce_sum.38), kind=kOutput, calls=%fused_computation.7 | convolution fusion | flops 20133314560 | bytes 56360960 | tf_op jit(solution)/shard_map/dot_general | solution.py:18
  590.4 14.3 %fusion.37 = f32[128,1792]{1,0:T(8,128)} fusion(f32[128,2560]{1,0:T(8,128)S(1)} %copy-done, f32[2560,1792]{1,0:T(8,128)} %param.9), kind=kOutput, calls=%fused_computation.69 | convolution fusion | flops 7046430720 | bytes 20578304 | tf_op jit(solution)/shard_map/dot_general | solution.py:18
  607.6 42.9 %all-reduce.12.cloned.1.call-done = f32[2560,128]{0,1:T(8,128)} async-done(((f32[2560,128]{0,1:T(8,128)}), f32[2560,128]{0,1:T(8,128)}) %all-reduce.12.cloned.1.call-update) | async-done | bytes 1310736 | tf_op jit(solution)/shard_map/psum | solution.py:47
  657.0 54.2 %all-reduce.14.cloned.1.call-done = (f32[128,128]{1,0:T(8,128)}, f32[128,128]{0,1:T(8,128)}, f32[128,1792]{1,0:T(8,128)}) async-done(((f32[128,128]{1,0:T(8,128)}, f32[128,128]{0,1:T(8,128)}, f32[128,1792]{1,0:T(8,128)}), (f32[128,128]{1,0:T(8,128)}, f32[128,128]{0,1:T(8,128)}, f32[128,1792]{1,0:T(8,128)})) %all-reduce.14.cloned.1.call-update) | async-done | bytes 1048592 | tf_op jit(solution)/shard_map/psum | solution.py:67
  712.6 11.7 %cholesky.81 = f32[128,128]{1,0:T(8,128)S(1)} custom-call(f32[128,128]{1,0:T(8,128)S(1)} %fusion.17), custom_call_target="Cholesky" | custom-call | tf_op jit(solution)/shard_map/jit(cholesky)/cholesky | solution.py:32
  725.7 9.8 %custom-call.11 = f32[1,128,128]{1,2,0:T(8,128)S(1)} custom-call(f32[1,128,128]{2,1,0:T(8,128)S(1)} %fusion.12), custom_call_target="InvertDiagBlocksLowerTriangular" | custom-call | tf_op jit(solution)/shard_map/jit(_cho_solve)/triangular_solve | solution.py:33
  739.0 17.4 %fusion.8 = f32[2560,1792]{1,0:T(8,128)} fusion(f32[2560,128]{0,1:T(8,128)S(1)} %convolution_add_fusion, f32[128,1792]{1,0:T(8,128)S(1)} %copy-done.5, f32[128,1792]{1,0:T(8,128)S(1)} %copy-done.6), kind=kOutput, calls=%fused_computation.21 | convolution fusion | flops 7046660096 | bytes 21495808 | tf_op jit(solution)/shard_map/dot_general | solution.py:18
  (76 shorter events, 42.1 us)
Async XLA Ops:
  6.5 37.8 %all-gather.10.cloned.1.call-start = ((), (), s32[]{:S(2)}) async-start(), calls=%async_computation | async-start | bytes 1638400 | tf_op jit(solution)/shard_map/all_gather | solution.py:51
  7.3 103.2 %all-gather.12.cloned.1.call-start = ((), (), s32[]{:S(2)}) async-start(), calls=%async_computation.4 | async-start | bytes 11796480 | tf_op jit(solution)/shard_map/all_gather | solution.py:8
  46.1 2.0 copy-start.2
  48.0 1.3 copy-start
  48.1 127.6 %all-gather.14.cloned.1.call-start = ((), (), s32[]{:S(2)}) async-start(), calls=%async_computation.5 | async-start | bytes 11796480 | tf_op jit(solution)/shard_map/all_gather | solution.py:8
  48.8 194.2 %all-reduce.10.cloned.1.call-start = ((), (), s32[]{:S(2)}) async-start(), calls=%async_computation.2 | async-start | bytes 131072 | tf_op jit(solution)/shard_map/psum | solution.py:53
  51.2 251.4 %all-reduce.8.cloned.1.call-start = ((), (), s32[]{:S(2)}) async-start(), calls=%async_computation.1 | async-start | bytes 2621440 | tf_op jit(solution)/shard_map/psum | solution.py:47
  242.4 119.4 %all-reduce.16.cloned.1.call-start = ((), (), s32[]{:S(2)}) async-start(), calls=%async_computation.9 | async-start | bytes 262144 | tf_op jit(solution)/shard_map/psum | solution.py:56
  307.0 79.6 %copy-start.4 = (f32[128,128]{1,0:T(8,128)S(1)}, f32[128,128]{1,0:T(8,128)}, u32[]{:S(2)}) copy-start(f32[128,128]{1,0:T(8,128)} %all-reduce.10.cloned.1.call-done) | copy-start | bytes 196612
  308.9 149.8 %all-gather.16.cloned.1.call-start = ((), (), s32[]{:S(2)}) async-start(), calls=%async_computation.6 | async-start | bytes 11796480 | tf_op jit(solution)/shard_map/all_gather | solution.py:8
  389.0 2.3 copy-start.3
  395.9 127.9 %all-gather.18.cloned.1.call-start = ((), (), s32[]{:S(2)}) async-start(), calls=%async_computation.7 | async-start | bytes 11796480 | tf_op jit(solution)/shard_map/all_gather | solution.py:8
  396.7 253.8 %all-reduce.12.cloned.1.call-start = ((), (), s32[]{:S(2)}) async-start(), calls=%async_computation.3 | async-start | bytes 2621440 | tf_op jit(solution)/shard_map/psum | solution.py:47
  590.3 14.4 %copy-start.1 = (f32[2560,128]{1,0:T(8,128)S(1)}, f32[2560,128]{1,0:T(8,128)}, u32[]{:S(2)}) copy-start(f32[2560,128]{1,0:T(8,128)} %get-tuple-element.16) | copy-start | bytes 3932164
  590.3 120.9 %all-reduce.14.cloned.1.call-start = ((), (), s32[]{:S(2)}) async-start(), calls=%async_computation.8 | async-start | bytes 2097152 | tf_op jit(solution)/shard_map/psum | solution.py:67
  736.2 2.8 copy-start.5
  736.2 2.8 copy-start.6
Sparse Core Ops, SparseCore 0:
  8.9 35.3 all-gather.9
  48.2 62.2 all-gather.11
  112.3 63.2 all-gather.13
  178.5 52.4 all-reduce.9
  242.5 60.0 all-reduce.7
  309.0 52.7 all-reduce.15
  396.0 62.6 all-gather.15
  460.6 63.2 all-gather.17
  590.5 59.9 all-reduce.11
  654.8 56.3 all-reduce.13
